TPU v7x, 512 devices: a whole 4x8x8 slice. The times are simulated.
512 devices in a mesh: fsdp: 128 (over z, y, core), seq: 4 (over x).
Axes of the slice: x: 4, y: 8, z: 8, core: 2. Of those that a mesh axis runs over, the one named last changes fastest.
Arguments:
- text_embeds: bfloat16 [35840, 4096], P('fsdp'), may hold values from -8 to 8
- vision_tokens: bfloat16 [16384, 4096], P('fsdp', 'seq'), may hold values from -6 to 6
- vision_request: int32 [16384, 1], P('fsdp'), may hold values from 0 to 127; in each aligned block of 128 rows (0 to 127, 128 to 255, ...) at most 2 rows name the same one
- image_start: int32 [128], P('fsdp'), may hold values from 1 to 16
- lengths: int32 [128], P('fsdp'), may hold values from 273 to 280
- attn_gain: float32 [4096], replicated, may hold values from 0.5 to 1.5
- w_query: bfloat16 [4096, 2048], P('fsdp', 'seq'), may hold values from -1 to 1
- w_key: bfloat16 [4096, 2048], P('fsdp', 'seq'), may hold values from -1 to 1
- w_value: bfloat16 [4096, 2048], P('fsdp', 'seq'), may hold values from -0.09375 to 0.09375
- w_out: bfloat16 [2048, 4096], P(None, 'fsdp'), may hold values from -0.125 to 0.125
- final_gain: float32 [4096], replicated, may hold values from 0.25 to 1.75
- lm_head: bfloat16 [4096, 32000], P(None, 'fsdp'), may hold values from -0.25 to 0.25
Outputs:
- state_rms: float32 [128], P('seq')
- max_logit: float32 [128], P('seq')
Inputs may be any that keep to these rules, and one draw needn't show every extreme that they name: `vision_request`: within the 128 vision tokens of one index of fsdp no request is named more than 2 times, a bound that some block reaches; every request is named by some vision token. `lengths`: each request's image tokens end before its last token.
All inputs are finite; a program needn't handle non-finite values.
Results may differ from a plain program's by a relative error of at most 0.0024.
Values may be sent and summed in bfloat16 or wider, within the bound.
No kernel may reach another device: no remote copies, remote signals or barrier semaphores. Data moves between devices by JAX's collectives and lax.ppermute only.
A program may use at most 128 MiB of HBM per device.

v0:
```python
import math
import jax
import jax.numpy as jnp
from jax import lax
from jax.sharding import PartitionSpec as P

HD = 128
norm_epsilon = 1e-05


def row_norm(rows, gain):
    widened = rows.astype(jnp.float32)
    return (
        widened
        * lax.rsqrt(jnp.mean(widened * widened, axis=1, keepdims=True) + norm_epsilon)
        * gain
    ).astype(jnp.bfloat16)


def exchange(rows, axis_name):
    return lax.all_to_all(rows, axis_name, split_axis=0, concat_axis=0, tiled=True)


def gather_by_exchange(piece, axis_name, count):
    spread = jnp.broadcast_to(piece[None], (count,) + piece.shape)
    return exchange(spread, axis_name)


def select_rows(selector, rows):
    return jnp.dot(selector.astype(jnp.bfloat16), rows, preferred_element_type=jnp.float32).astype(
        jnp.bfloat16
    )


def local(
    text_embeds,
    vision_tokens,
    vision_request,
    image_start,
    lengths,
    attn_gain,
    w_query,
    w_key,
    w_value,
    w_out,
    final_gain,
    lm_head,
):
    groups = lax.axis_size("fsdp")
    seq_count = lax.axis_size("seq")
    seq_index = lax.axis_index("seq")
    seq_len = text_embeds.shape[0]
    width = text_embeds.shape[1]
    columns = w_key.shape[1]
    heads_local = columns // HD
    dpiece = width // groups
    quarter = groups // seq_count
    capacity = max(2, 2 * vision_tokens.shape[0] // groups)
    last_index = lengths[0] - 1
    destination = vision_request[:, 0]
    onehot = (destination[:, None] == jnp.arange(groups, dtype=jnp.int32)[None, :]).astype(
        jnp.int32
    )
    slot_index = jnp.sum((jnp.cumsum(onehot, axis=0) - onehot) * onehot, axis=1)
    counts = jnp.sum(onehot, axis=0)
    final_text = lax.dynamic_slice_in_dim(text_embeds, last_index, 1, 0)
    last_normed = row_norm(final_text, attn_gain)
    pieces = jnp.stack(
        [
            final_text.reshape(groups, dpiece),
            last_normed.reshape(groups, dpiece),
            jnp.broadcast_to(counts.astype(jnp.bfloat16)[:, None], (groups, dpiece)),
        ],
        axis=1,
    )
    pieces_in = exchange(pieces, "fsdp")
    text_part = pieces_in[:, 0]
    normed_part = pieces_in[:, 1]
    arrived = pieces_in[:, 2, :1].astype(jnp.int32)
    query_partial = jnp.dot(normed_part, w_query, preferred_element_type=jnp.float32)
    query_all = lax.psum(query_partial, "fsdp").astype(jnp.bfloat16)
    query_heads = query_all.astype(jnp.float32).reshape(groups, heads_local, HD)
    key_rows = w_key.astype(jnp.float32).reshape(dpiece, heads_local, HD)
    probe_part = jnp.einsum("rhc,dhc->rhd", query_heads, key_rows, precision=lax.Precision.HIGHEST)
    probe_in = exchange(probe_part, "fsdp")
    probe = jnp.transpose(probe_in, (1, 0, 2)).reshape(heads_local, width)
    full_vision = lax.all_gather(vision_tokens, "seq", axis=1, tiled=True)
    slot_of = destination * capacity + slot_index
    outbox_select = jnp.arange(groups * capacity, dtype=jnp.int32)[:, None] == slot_of[None, :]
    outbox = select_rows(outbox_select, full_vision).reshape(groups, capacity, width)
    received = exchange(outbox, "fsdp")
    occupied = (
        (jnp.arange(capacity, dtype=jnp.int32)[None, :] < arrived).astype(jnp.int32).reshape(-1)
    )
    ranking = jnp.cumsum(occupied) - occupied
    positions = jnp.where(occupied > 0, image_start[0] + ranking, seq_len)
    place = jnp.arange(seq_len, dtype=jnp.int32)[:, None] == positions[None, :]
    placed = select_rows(place, received.reshape(-1, width))
    replaced = jnp.any(place, axis=1, keepdims=True)
    states = jnp.where(replaced, placed, text_embeds)
    normed = row_norm(states, attn_gain)
    scores = jnp.dot(
        normed.astype(jnp.float32), probe.T, precision=lax.Precision.HIGHEST
    ).T / math.sqrt(HD)
    live_keys = jnp.arange(seq_len, dtype=jnp.int32) < lengths[0]
    scores = jnp.where(live_keys[None, :], scores, -jnp.inf)
    peak = jnp.max(scores, axis=1, keepdims=True)
    shifted = jnp.exp(scores - peak)
    weights = (shifted / jnp.sum(shifted, axis=1, keepdims=True)).astype(jnp.bfloat16)
    mixed = jnp.dot(weights, normed, preferred_element_type=jnp.float32)
    mixed_pieces = jnp.transpose(mixed.reshape(heads_local, groups, dpiece), (1, 0, 2))
    mixed_in = exchange(mixed_pieces, "fsdp")
    value_rows = w_value.astype(jnp.float32).reshape(dpiece, heads_local, HD)
    attended_partial = jnp.einsum(
        "rhd,dhc->rhc", mixed_in, value_rows, precision=lax.Precision.HIGHEST
    ).reshape(groups, columns)
    attended_seq = lax.psum(attended_partial, "fsdp").astype(jnp.bfloat16)
    out_rows = lax.dynamic_slice_in_dim(w_out, seq_index * columns, columns, 0)
    partial_out = jnp.dot(attended_seq, out_rows, preferred_element_type=jnp.float32)
    out_mine = lax.psum_scatter(partial_out, "seq", scatter_dimension=0, tiled=True)
    text_mine = lax.dynamic_slice_in_dim(text_part, seq_index * quarter, quarter, 0)
    residual_out = text_mine.astype(jnp.float32) + out_mine
    residual_all = gather_by_exchange(residual_out, "fsdp", groups)
    last_state = jnp.transpose(residual_all, (1, 0, 2)).reshape(quarter, width)
    mean_square = jnp.mean(last_state * last_state, axis=1)
    scaled_out = (last_state * final_gain[None, :]).astype(jnp.bfloat16)
    logits = jnp.dot(scaled_out, lm_head, preferred_element_type=jnp.float32)
    local_max = jnp.max(logits, axis=1) * lax.rsqrt(mean_square + norm_epsilon)
    max_all = gather_by_exchange(local_max, "fsdp", groups)
    max_logit = jnp.max(max_all, axis=0)
    return (jnp.sqrt(mean_square), max_logit)


def solution(mesh):
    return jax.shard_map(
        local,
        mesh=mesh,
        in_specs=(
            P("fsdp", None),
            P("fsdp", "seq"),
            P("fsdp", None),
            P("fsdp"),
            P("fsdp"),
            P(),
            P("fsdp", "seq"),
            P("fsdp", "seq"),
            P("fsdp", "seq"),
            P(None, "fsdp"),
            P(),
            P(None, "fsdp"),
        ),
        out_specs=(P("seq"), P("seq")),
        check_vma=False,
    )
```

profile of v0, /device:TPU:1, one launch (start us, length us, event | category | flops | bytes accessed | tf_op | source)
XLA Modules:
  0.0 1239.9 jit_solution(17929459743585523007)
XLA Ops:
  14.5 18.4 %all-to-all-start = ((bf16[128,3,32]{2,1,0:T(4,128)(2,1)}), bf16[128,3,32]{2,1,0:T(4,128)(2,1)S(1)}, u32[]{:S(2)}, u32[]{:S(2)}) async-start(bf16[128,3,32]{2,1,0:T(4,128)(2,1)} %copy.59), calls=%async_computation | async-start | bytes 262144 | tf_op jit(solution)/shard_map/all_to_all | solution.py:21
  33.6 12.1 all-to-all-done
  46.8 485.9 %all-reduce.2 = bf16[128,512]{1,0:T(8,128)(2,1)S(1)} all-reduce(f32[128,512]{1,0:T(8,128)S(1)} %fusion.27), channel_id=1, replica_groups=mesh['fsdp'=128,'seq'=4] {'fsdp'}, use_global_device_ids=true, to_apply=%region_2.3 | all-reduce | flops 65536 | bytes 393216 | tf_op jit(solution)/shard_map/psum | solution.py:81
  533.8 11.7 all-to-all-start.1
  545.6 3.2 convolution_convert_fusion.1
  548.8 4.4 reshape.146
  553.2 3.8 all-to-all-done.1
  557.0 10.4 all-to-all-start.2
  568.2 2.4 fusion.17
  573.6 44.7 %all-to-all-done.2 = bf16[128,2,4096]{2,1,0:T(2,128)(2,1)} async-done(((bf16[128,2,4096]{2,1,0:T(2,128)(2,1)}), bf16[128,2,4096]{2,1,0:T(2,128)(2,1)}, u32[]{:S(2)}, u32[]{:S(2)}) %all-to-all-start.2) | async-done | bytes 2097184 | tf_op jit(solution)/shard_map/all_to_all | solution.py:21
  618.3 4.1 reshape.147
  622.4 3.3 fusion.1
  625.8 2.1 fusion.36
  630.0 8.9 all-to-all-start.3
  639.0 11.4 all-to-all-done.3
  651.8 486.1 %all-reduce.3 = bf16[128,512]{0,1:T(8,128)(2,1)S(1)} all-reduce(f32[128,512]{0,1:T(8,128)S(1)} %bitcast.64), channel_id=1, replica_groups=mesh['fsdp'=128,'seq'=4] {'fsdp'}, use_global_device_ids=true, to_apply=%region_11.12 | all-reduce | flops 65536 | bytes 393216 | tf_op jit(solution)/shard_map/psum | solution.py:117
  1139.5 22.1 %reduce-scatter.2.cloned.1.call-done = f32[32,32]{1,0:T(8,128)} async-done(((f32[128,32]{1,0:T(8,128)}), f32[32,32]{1,0:T(8,128)}) %reduce-scatter.2.cloned.1.call-update) | async-done | bytes 4112 | tf_op jit(solution)/shard_map/reduce_scatter | solution.py:120
  1164.0 2.5 reshape.165
  1166.5 36.9 %all_to_all.31 = f32[128,1,1024]{2,1,0:T(1,128)S(1)} all-to-all(f32[128,1,1024]{2,1,0:T(1,128)S(1)} %reshape.165), channel_id=1, replica_groups=mesh['fsdp'=128,'seq'=4] {'fsdp'}, dimensions={0} | all-to-all | bytes 1048576 | tf_op jit(solution)/shard_map/all_to_all | solution.py:21
  1205.3 2.0 reshape.166
  1207.3 2.1 multiply_reduce_fusion
  1209.5 2.6 copy.69
  1212.1 2.6 reshape.151
  1215.8 16.7 %all_to_all.32 = f32[128,1,32]{2,1,0:T(1,128)S(1)} all-to-all(f32[128,1,32]{2,1,0:T(1,128)S(1)} %broadcast_in_dim.36), channel_id=1, replica_groups=mesh['fsdp'=128,'seq'=4] {'fsdp'}, dimensions={0} | all-to-all | bytes 32768 | tf_op jit(solution)/shard_map/all_to_all | solution.py:21
  (73 shorter events, 23.3 us)
Async XLA Ops:
  7.2 1207.5 %copy-start = (bf16[4096,250]{1,0:T(8,128)(2,1)S(1)}, bf16[4096,250]{1,0:T(8,128)(2,1)}, u32[]{:S(2)}) copy-start(bf16[4096,250]{1,0:T(8,128)(2,1)} %param.23) | copy-start | bytes 6144004
  7.2 525.5 %copy-start.2 = (bf16[32,512]{1,0:T(8,128)(2,1)S(1)}, bf16[32,512]{1,0:T(8,128)(2,1)}, u32[]{:S(2)}) copy-start(bf16[32,512]{1,0:T(8,128)(2,1)} %param.19) | copy-start | bytes 98308
  7.2 538.4 %all-gather.2.cloned.1.call-start = ((), (), s32[]{:S(2)}) async-start(), calls=%async_computation.7 | async-start | bytes 1310720 | tf_op jit(solution)/shard_map/all_gather | solution.py:87
  14.5 31.2 %all-to-all-start = ((bf16[128,3,32]{2,1,0:T(4,128)(2,1)}), bf16[128,3,32]{2,1,0:T(4,128)(2,1)S(1)}, u32[]{:S(2)}, u32[]{:S(2)}) async-start(bf16[128,3,32]{2,1,0:T(4,128)(2,1)} %copy.59), calls=%async_computation | async-start | bytes 262144 | tf_op jit(solution)/shard_map/all_to_all | solution.py:21
  533.8 23.2 %all-to-all-start.1 = ((f32[128,1,128]{2,1,0:T(1,128)}), f32[128,1,128]{2,1,0:T(1,128)S(1)}, u32[]{:S(2)}, u32[]{:S(2)}) async-start(f32[128,1,128]{2,1,0:T(1,128)} %reshape.161), calls=%async_computation.1 | async-start | bytes 131072 | tf_op jit(solution)/shard_map/all_to_all | solution.py:21
  557.0 61.3 %all-to-all-start.2 = ((bf16[128,2,4096]{2,1,0:T(2,128)(2,1)}), bf16[128,2,4096]{2,1,0:T(2,128)(2,1)}, u32[]{:S(2)}, u32[]{:S(2)}) async-start(bf16[128,2,4096]{2,1,0:T(2,128)(2,1)} %reshape.146), calls=%async_computation.2 | async-start | bytes 4194304 | tf_op jit(solution)/shard_map/all_to_all | solution.py:21
  622.4 3.4 copy-start.5
  628.1 23.3 %copy-start.3 = (bf16[32,512]{1,0:T(8,128)(2,1)S(1)}, bf16[32,512]{1,0:T(8,128)(2,1)}, u32[]{:S(2)}) copy-start(bf16[32,512]{1,0:T(8,128)(2,1)} %param.20) | copy-start | bytes 98308
  630.0 20.4 %all-to-all-start.3 = ((f32[128,1,128]{2,1,0:T(1,128)}), f32[128,1,128]{2,1,0:T(1,128)S(1)}, u32[]{:S(2)}, u32[]{:S(2)}) async-start(f32[128,1,128]{2,1,0:T(1,128)} %reshape.163), calls=%async_computation.3 | async-start | bytes 131072 | tf_op jit(solution)/shard_map/all_to_all | solution.py:21
  639.0 522.7 %reduce-scatter.2.cloned.1.call-start = ((), (), s32[]{:S(2)}) async-start(), calls=%async_computation.8 | async-start | bytes 81920 | tf_op jit(solution)/shard_map/reduce_scatter | solution.py:120
  1207.3 2.2 copy-start.1
  1212.1 2.6 copy-start.4
Sparse Core Ops, SparseCore 0:
  10.1 33.8 all-gather.1
  1139.6 21.9 reduce-scatter.1
where the time goes:
time: 1240 us
  blocking collectives  1030 us (83%)
  waiting for transfers between devices  94.8 us (8%)
  starting transfers between devices  49.6 us (4%)
  local copies, waits for them, and re-layouts  25.1 us (2%)
  between operations  16.3 us (1%)
  other arithmetic  15.6 us (1%)
  matrix products  13.1 us (1%)
    psum x1, blocking collectives, local(): attended_seq = lax.psum(attended_partial, 'fsdp').astype(jnp.bfloat16)  486 us
    psum x1, blocking collectives, local(): query_all = lax.psum(query_partial, 'fsdp').astype(jnp.bfloat16)  486 us
    all_to_all x4, waiting for transfers between devices, exchange(): lax.all_to_all(rows, axis_name, split_axis=0, concat_axis=0, tiled=True)  72 us
    all_to_all x2, blocking collectives, exchange(): lax.all_to_all(rows, axis_name, split_axis=0, concat_axis=0, tiled=True)  53.6 us
    all_to_all x4, starting transfers between devices, exchange(): lax.all_to_all(rows, axis_name, split_axis=0, concat_axis=0, tiled=True)  49.5 us
  transfers between devices with their start and end apart: 6, of which 5 were waited for; matrix products, arithmetic and copies ran while one was open for 2% of the time, Pallas kernels for 0%

commit v1 on v0

--- a/solution.py
+++ b/solution.py
@@ -78,7 +78,7 @@
     normed_part = pieces_in[:, 1]
     arrived = pieces_in[:, 2, :1].astype(jnp.int32)
     query_partial = jnp.dot(normed_part, w_query, preferred_element_type=jnp.float32)
-    query_all = lax.psum(query_partial, "fsdp").astype(jnp.bfloat16)
+    query_all = jnp.sum(lax.all_gather(query_partial, "fsdp"), axis=0).astype(jnp.bfloat16)
     query_heads = query_all.astype(jnp.float32).reshape(groups, heads_local, HD)
     key_rows = w_key.astype(jnp.float32).reshape(dpiece, heads_local, HD)
     probe_part = jnp.einsum("rhc,dhc->rhd", query_heads, key_rows, precision=lax.Precision.HIGHEST)

time: 1240 us -> 879 us (0.71)
  blocking collectives: 1030 us -> 571 us
  waiting for transfers between devices: 94.8 us -> 194 us
  starting transfers between devices: 49.6 us -> 29.2 us
    psum x1 -> x0, blocking collectives: 486 us -> none  [local(): query_all = lax.psum(query_partial, 'fsdp').astype(jnp.bfloat16)]
    all_gather x0 -> x1, waiting for transfers between devices: none -> 96.5 us  [local(): lax.all_gather(query_partial, 'fsdp')]
    all_to_all x2 -> x3, blocking collectives: 53.6 us -> 84.5 us  [exchange(): lax.all_to_all(rows, axis_name, split_axis=0, concat_axis=0, tiled=True)]
    all_to_all x4 -> x3, starting transfers between devices: 49.5 us -> 29.1 us  [exchange(): lax.all_to_all(rows, axis_name, split_axis=0, concat_axis=0, tiled=True)]
    all_to_all x4 -> x3, waiting for transfers between devices: 72 us -> 74.8 us  [exchange(): lax.all_to_all(rows, axis_name, split_axis=0, concat_axis=0, tiled=True)]
  transfers between devices with their start and end apart: 6 -> 6, of which waited for: 5 -> 5; matrix products, arithmetic and copies ran while one was open for 2% -> 3% of each run, Pallas kernels for 0% -> 0%
where the time goes in v1:
time: 879 us; the launch traced here: 878 us
  blocking collectives  571 us (65%)
  waiting for transfers between devices  194 us (22%)
  starting transfers between devices  29.2 us (3%)
  other arithmetic  26.9 us (3%)
  local copies, waits for them, and re-layouts  24.5 us (3%)
  matrix products  16.9 us (2%)
  between operations  16.1 us (2%)
    psum x1, blocking collectives, local(): attended_seq = lax.psum(attended_partial, 'fsdp').astype(jnp.bfloat16)  486 us
    all_gather x1, waiting for transfers between devices, local(): lax.all_gather(query_partial, 'fsdp')  96.5 us
    all_to_all x3, blocking collectives, exchange(): lax.all_to_all(rows, axis_name, split_axis=0, concat_axis=0, tiled=True)  84.5 us
    all_to_all x3, waiting for transfers between devices, exchange(): lax.all_to_all(rows, axis_name, split_axis=0, concat_axis=0, tiled=True)  74.8 us
    all_to_all x3, starting transfers between devices, exchange(): lax.all_to_all(rows, axis_name, split_axis=0, concat_axis=0, tiled=True)  29.1 us
    reduce_scatter x1, waiting for transfers between devices, local(): lax.psum_scatter(partial_out, 'seq', scatter_dimension=0, tiled=True)  22 us
  transfers between devices with their start and end apart: 6, of which 5 were waited for; matrix products, arithmetic and copies ran while one was open for 3% of the time, Pallas kernels for 0%

profile of v1, /device:TPU:1, one launch (start us, length us, event | category | flops | bytes accessed | tf_op | source)
XLA Modules:
  0.0 878.3 jit_solution(13817283674888543951)
XLA Ops:
  13.9 31.0 %all_to_all.31 = bf16[128,3,32]{2,1,0:T(4,128)(2,1)S(1)} all-to-all(bf16[128,3,32]{2,1,0:T(4,128)(2,1)S(1)} %copy.61), channel_id=1, replica_groups=mesh['fsdp'=128,'seq'=4] {'fsdp'}, dimensions={0} | all-to-all | bytes 49152 | tf_op jit(solution)/shard_map/all_to_all | solution.py:21
  46.8 3.2 convolution_convert_fusion.1
  50.0 4.4 reshape.145
  54.5 12.9 %all-to-all-start.2 = ((bf16[128,2,4096]{2,1,0:T(2,128)(2,1)}), bf16[128,2,4096]{2,1,0:T(2,128)(2,1)}, u32[]{:S(2)}, u32[]{:S(2)}) async-start(bf16[128,2,4096]{2,1,0:T(2,128)(2,1)} %reshape.145), calls=%async_computation.2 | async-start | bytes 4194304 | tf_op jit(solution)/shard_map/all_to_all | solution.py:21
  68.2 2.4 fusion.15
  71.8 51.9 %all-to-all-done.2 = bf16[128,2,4096]{2,1,0:T(2,128)(2,1)} async-done(((bf16[128,2,4096]{2,1,0:T(2,128)(2,1)}), bf16[128,2,4096]{2,1,0:T(2,128)(2,1)}, u32[]{:S(2)}, u32[]{:S(2)}) %all-to-all-start.2) | async-done | bytes 2097184 | tf_op jit(solution)/shard_map/all_to_all | solution.py:21
  123.7 4.1 reshape.146
  127.8 4.6 fusion.1
  132.5 96.5 %all-gather.6.cloned.1.call-done = f32[16384,512]{1,0:T(8,128)} async-done(((f32[128,512]{1,0:T(8,128)}), f32[16384,512]{1,0:T(8,128)}) %all-gather.6.cloned.1.call-update) | async-done | bytes 33554448 | tf_op jit(solution)/shard_map/all_gather | solution.py:81
  228.9 12.0 %reduce_sum.65 = bf16[128,512]{1,0:T(8,128)(2,1)S(1)} reduce(f32[128,128,512]{2,1,0:T(8,128)} %bitcast.55, f32[]{:T(128)} %constant.19.clone.1), dimensions={0}, to_apply=%region_2.3 | reduce | flops 8323072 | bytes 33685508 | tf_op jit(solution)/shard_map/reduce_sum | solution.py:81
  242.2 10.5 %all-to-all-start.1 = ((f32[128,1,128]{2,1,0:T(1,128)}), f32[128,1,128]{2,1,0:T(1,128)S(1)}, u32[]{:S(2)}, u32[]{:S(2)}) async-start(f32[128,1,128]{2,1,0:T(1,128)} %reshape.161), calls=%async_computation.1 | async-start | bytes 131072 | tf_op jit(solution)/shard_map/all_to_all | solution.py:21
  252.7 11.4 %all-to-all-done.1 = f32[128,1,128]{2,1,0:T(1,128)S(1)} async-done(((f32[128,1,128]{2,1,0:T(1,128)}), f32[128,1,128]{2,1,0:T(1,128)S(1)}, u32[]{:S(2)}, u32[]{:S(2)}) %all-to-all-start.1) | async-done | bytes 65568 | tf_op jit(solution)/shard_map/all_to_all | solution.py:21
  265.8 3.9 fusion.34
  271.8 5.8 all-to-all-start.3
  277.6 11.5 %all-to-all-done.3 = f32[128,1,128]{2,1,0:T(1,128)S(1)} async-done(((f32[128,1,128]{2,1,0:T(1,128)}), f32[128,1,128]{2,1,0:T(1,128)S(1)}, u32[]{:S(2)}, u32[]{:S(2)}) %all-to-all-start.3) | async-done | bytes 65568 | tf_op jit(solution)/shard_map/all_to_all | solution.py:21
  290.6 486.1 %all-reduce.1 = bf16[128,512]{0,1:T(8,128)(2,1)S(1)} all-reduce(f32[128,512]{0,1:T(8,128)S(1)} %bitcast.59), channel_id=1, replica_groups=mesh['fsdp'=128,'seq'=4] {'fsdp'}, use_global_device_ids=true, to_apply=%region_11.12 | all-reduce | flops 65536 | bytes 393216 | tf_op jit(solution)/shard_map/psum | solution.py:117
  778.3 22.0 %reduce-scatter.2.cloned.1.call-done = f32[32,32]{1,0:T(8,128)} async-done(((f32[128,32]{1,0:T(8,128)}), f32[32,32]{1,0:T(8,128)}) %reduce-scatter.2.cloned.1.call-update) | async-done | bytes 4112 | tf_op jit(solution)/shard_map/reduce_scatter | solution.py:120
  802.7 2.5 reshape.165
  805.2 36.9 %all_to_all.32 = f32[128,1,1024]{2,1,0:T(1,128)S(1)} all-to-all(f32[128,1,1024]{2,1,0:T(1,128)S(1)} %reshape.165), channel_id=1, replica_groups=mesh['fsdp'=128,'seq'=4] {'fsdp'}, dimensions={0} | all-to-all | bytes 1048576 | tf_op jit(solution)/shard_map/all_to_all | solution.py:21
  843.9 2.0 reshape.166
  846.0 2.1 multiply_reduce_fusion
  848.2 2.6 copy.72
  850.8 2.6 reshape.150
  854.5 16.7 %all_to_all.33 = f32[128,1,32]{2,1,0:T(1,128)S(1)} all-to-all(f32[128,1,32]{2,1,0:T(1,128)S(1)} %broadcast_in_dim.36), channel_id=1, replica_groups=mesh['fsdp'=128,'seq'=4] {'fsdp'}, dimensions={0} | all-to-all | bytes 32768 | tf_op jit(solution)/shard_map/all_to_all | solution.py:21
  (80 shorter events, 22.8 us)
Async XLA Ops:
  7.2 846.2 %copy-start = (bf16[4096,250]{1,0:T(8,128)(2,1)S(1)}, bf16[4096,250]{1,0:T(8,128)(2,1)}, u32[]{:S(2)}) copy-start(bf16[4096,250]{1,0:T(8,128)(2,1)} %param.23) | copy-start | bytes 6144004
  7.2 39.6 %copy-start.6 = (s32[128,1]{0,1:T(1,128)S(1)}, s32[128,1]{0,1:T(1,128)}, u32[]{:S(2)}) copy-start(s32[128,1]{0,1:T(1,128)} %param.14) | copy-start | bytes 1540
  7.2 39.6 %all-gather.4.cloned.1.call-start = ((), (), s32[]{:S(2)}) async-start(), calls=%async_computation.7 | async-start | bytes 1310720 | tf_op jit(solution)/shard_map/all_gather | solution.py:87
  7.9 221.0 %all-gather.6.cloned.1.call-start = ((), (), s32[]{:S(2)}) async-start(), calls=%async_computation.9 | async-start | bytes 33816576 | tf_op jit(solution)/shard_map/all_gather | solution.py:81
  54.5 69.3 %all-to-all-start.2 = ((bf16[128,2,4096]{2,1,0:T(2,128)(2,1)}), bf16[128,2,4096]{2,1,0:T(2,128)(2,1)}, u32[]{:S(2)}, u32[]{:S(2)}) async-start(bf16[128,2,4096]{2,1,0:T(2,128)(2,1)} %reshape.145), calls=%async_computation.2 | async-start | bytes 4194304 | tf_op jit(solution)/shard_map/all_to_all | solution.py:21
  228.9 12.1 %copy-start.2 = (bf16[32,512]{1,0:T(8,128)(2,1)S(1)}, bf16[32,512]{1,0:T(8,128)(2,1)}, u32[]{:S(2)}) copy-start(bf16[32,512]{1,0:T(8,128)(2,1)} %param.19) | copy-start | bytes 98308
  240.9 24.9 %copy-start.5 = (f32[4096]{0:T(1024)S(1)}, f32[4096]{0:T(1024)}, u32[]{:S(2)}) copy-start(f32[4096]{0:T(1024)} %param.17) | copy-start | bytes 49156
  242.2 21.9 %all-to-all-start.1 = ((f32[128,1,128]{2,1,0:T(1,128)}), f32[128,1,128]{2,1,0:T(1,128)S(1)}, u32[]{:S(2)}, u32[]{:S(2)}) async-start(f32[128,1,128]{2,1,0:T(1,128)} %reshape.161), calls=%async_computation.1 | async-start | bytes 131072 | tf_op jit(solution)/shard_map/all_to_all | solution.py:21
  265.8 4.1 copy-start.7
  269.9 20.2 %copy-start.3 = (bf16[32,512]{1,0:T(8,128)(2,1)S(1)}, bf16[32,512]{1,0:T(8,128)(2,1)}, u32[]{:S(2)}) copy-start(bf16[32,512]{1,0:T(8,128)(2,1)} %param.20) | copy-start | bytes 98308
  271.8 17.3 %all-to-all-start.3 = ((f32[128,1,128]{2,1,0:T(1,128)}), f32[128,1,128]{2,1,0:T(1,128)S(1)}, u32[]{:S(2)}, u32[]{:S(2)}) async-start(f32[128,1,128]{2,1,0:T(1,128)} %reshape.163), calls=%async_computation.3 | async-start | bytes 131072 | tf_op jit(solution)/shard_map/all_to_all | solution.py:21
  277.6 522.7 %reduce-scatter.2.cloned.1.call-start = ((), (), s32[]{:S(2)}) async-start(), calls=%async_computation.8 | async-start | bytes 81920 | tf_op jit(solution)/shard_map/reduce_scatter | solution.py:120
  846.0 2.2 copy-start.1
  850.8 2.6 copy-start.4
Sparse Core Ops, SparseCore 0:
  10.1 33.8 all-gather.3
  47.2 181.7 all-gather.5
  778.4 21.9 reduce-scatter.1
